TPU v7x, 128 devices: a whole 4x4x4 slice. The times are simulated.
128 devices in a mesh: section: 4 (over x), dp: 32 (over y, z, core).
Axes of the slice: x: 4, y: 4, z: 4, core: 2. Of those that a mesh axis runs over, the one named last changes fastest.
Arguments:
- tokens: bfloat16 [4096, 8192], P('dp'), may hold values from -6 to 6
- cotangent: bfloat16 [4096, 8192], P('dp'), may hold values from -6 to 6
- gains: float32 [4, 8192], P('section'), may hold values from 0.5 to 1.5
- value_projection_weight: bfloat16 [4, 8192, 1024], P('section', 'dp'), may hold values from -0.0625 to 0.0625
- output_projection_weight: bfloat16 [4, 8192, 1024], P('section', 'dp'), may hold values from -0.1875 to 0.1875
- block_adapter_ids: int32 [32], replicated, may hold values from 0 to 63
- job_adapter: int32 [32, 64], replicated, may hold values from -1 to 63, as said below
- job_slab: int32 [32, 64], replicated, may hold values from -1 to 15, as said below
- token_counts: int32 [64], replicated, may hold values from 128 to 1023
- slot_adapter_params: bfloat16 [4, 2048, 9216], P('section', 'dp'), may hold values from -0.29882812 to 0.29882812
- first_moment: float32 [4, 2048, 9216], P('section', 'dp'), may hold values from -6 to 6
- second_moment: float32 [4, 2048, 9216], P('section', 'dp'), may hold values from 0.1 to 10
Outputs:
- new_params: bfloat16 [4, 2048, 9216], P('section', 'dp')
- new_first: float32 [4, 2048, 9216], P('section', 'dp')
- new_second: float32 [4, 2048, 9216], P('section', 'dp')
- user_panels: bfloat16 [4, 32, 147456], P('section', 'dp')
Inputs may be any that keep to these rules, and one draw needn't show every extreme that they name: `job_adapter`: row o lists the adapters of which owner o holds a slab, each once, followed by -1; the 16 slabs of every adapter are held by 16 different owners, and every slab of every adapter is held exactly once. `job_slab`: the slab held in the same entry of job_adapter; -1 exactly where job_adapter is -1.
All inputs are finite; a program needn't handle non-finite values.
Results may differ from a plain program's by a relative error of at most 0.001.
Values may be sent and summed in bfloat16 or wider, within the bound.
No kernel may reach another device: no remote copies, remote signals or barrier semaphores. Data moves between devices by JAX's collectives and lax.ppermute only.
A program may use at most 128 MiB of HBM per device.

v0:
```python
import jax
import jax.numpy as jnp
from jax import lax
from jax.sharding import PartitionSpec as P

ADAPTER_RANK = 16
MROWS = 16
ADAPTER_SCALE = 2.0
LEARN_RATE = 0.001
BETA_FIRST = 0.9
BETA_SECOND = 0.999
ADAM_EPS = 1e-08
FIRST_FIX = 1.0 - 0.9**50 * 0.9**50
SECOND_FIX = 1.0 - 0.999**50 * 0.999**50
NORM_EPS = 1e-05


def from_behind(shard, axis, by):
    length = lax.axis_size(axis)
    pairs = [(i, i + by) for i in range(length) if 0 <= i + by < length]
    return lax.ppermute(shard, axis, pairs)


def contract_trailing(left, right):
    return lax.dot_general(
        left, right, (((1,), (1,)), ((), ())), preferred_element_type=jnp.float32
    )


def contract_leading(left, right):
    return lax.dot_general(
        left, right, (((0,), (0,)), ((), ())), preferred_element_type=jnp.float32
    )


def norm_rows(hidden_state, gain_vector_row):
    hidden_wide = hidden_state.astype(jnp.float32)
    mean_square = jnp.mean(hidden_wide * hidden_wide, axis=-1, keepdims=True)
    norm_gain_scale = lax.rsqrt(mean_square + NORM_EPS)
    normalized_rows = (hidden_wide * norm_gain_scale * gain_vector_row).astype(jnp.bfloat16)
    return (hidden_wide, norm_gain_scale, normalized_rows)


def layer_ahead_pass(
    hidden_state, gain_vector_row, value_complete, output_complete, adapter_down, adapter_up
):
    hidden_wide, norm_gain_scale, normalized_rows = norm_rows(hidden_state, gain_vector_row)
    rank_projected = jnp.dot(
        normalized_rows, adapter_down, preferred_element_type=jnp.float32
    ).astype(jnp.bfloat16)
    value_block_rows = (
        jnp.dot(normalized_rows, value_complete, preferred_element_type=jnp.float32)
        + ADAPTER_SCALE * jnp.dot(rank_projected, adapter_up, preferred_element_type=jnp.float32)
    ).astype(jnp.bfloat16)
    output_block_rows = (hidden_wide + contract_trailing(value_block_rows, output_complete)).astype(
        jnp.bfloat16
    )
    return (output_block_rows, norm_gain_scale, normalized_rows, rank_projected)


def layer_reverse_pass(
    output_gradient,
    hidden_state,
    norm_gain_scale,
    normalized_rows,
    rank_projected,
    gain_vector_row,
    value_complete,
    output_complete,
    adapter_down,
    adapter_up,
):
    value_gradient = jnp.dot(
        output_gradient, output_complete, preferred_element_type=jnp.float32
    ).astype(jnp.bfloat16)
    low_rank_gradient = (ADAPTER_SCALE * contract_trailing(value_gradient, adapter_up)).astype(
        jnp.bfloat16
    )
    down_gradient = contract_leading(normalized_rows, low_rank_gradient)
    up_gradient = ADAPTER_SCALE * contract_leading(rank_projected, value_gradient)
    normed_gradient = (
        contract_trailing(value_gradient, value_complete)
        + contract_trailing(low_rank_gradient, adapter_down)
    ) * gain_vector_row
    hidden_wide = hidden_state.astype(jnp.float32)
    centred = jnp.mean(hidden_wide * normed_gradient, axis=-1, keepdims=True)
    grad_in = (
        output_gradient.astype(jnp.float32)
        + norm_gain_scale * normed_gradient
        - hidden_wide * norm_gain_scale**3 * centred
    )
    return (grad_in.astype(jnp.bfloat16), down_gradient, up_gradient)


def adam_update(params_old, first_old, second_old, slot_grad, live):
    first_step = BETA_FIRST * first_old + (1.0 - BETA_FIRST) * slot_grad
    second_step = BETA_SECOND * second_old + (1.0 - BETA_SECOND) * slot_grad * slot_grad
    step_size = first_step / FIRST_FIX / (jnp.sqrt(second_step / SECOND_FIX) + ADAM_EPS)
    params_step = (params_old.astype(jnp.float32) - LEARN_RATE * step_size).astype(jnp.bfloat16)
    return (
        jnp.where(live, params_step, params_old),
        jnp.where(live, first_step, first_old),
        jnp.where(live, second_step, second_old),
    )


def put_slot(saved_array, new_value, slot_number, is_valid):
    current = lax.dynamic_index_in_dim(saved_array, slot_number, 0, keepdims=False)
    return lax.dynamic_update_index_in_dim(
        saved_array, jnp.where(is_valid, new_value, current), slot_number, 0
    )


def select_slot(saved_array, slot_number):
    return lax.dynamic_index_in_dim(saved_array, slot_number, 0, keepdims=False)


def on_device(
    tokens,
    cotangent,
    gains,
    value_projection_weight,
    output_projection_weight,
    block_adapter_ids,
    job_adapter,
    job_slab,
    token_counts,
    slot_adapter_params,
    first_moment,
    second_moment,
):
    section_index = lax.axis_index("section")
    owner_index = lax.axis_index("dp")
    section_total = lax.axis_size("section")
    owner_total = lax.axis_size("dp")
    tok_dev, hidden_width = tokens.shape
    value_feature_width = value_projection_weight.shape[2]
    panel_width = slot_adapter_params.shape[2]
    slab_count = owner_total // 2
    block_total = block_adapter_ids.shape[0]
    local_blocks = block_total // owner_total
    block_rows = tok_dev // local_blocks
    adapter_total = token_counts.shape[0]
    divide_position = hidden_width * ADAPTER_RANK
    value_complete, output_complete = (
        lax.all_gather(value_projection_weight, "dp", axis=1, tiled=True),
        lax.all_gather(output_projection_weight, "dp", axis=1, tiled=True),
    )
    value_complete = value_complete[0]
    output_complete = output_complete[0]
    gain_vector_row = gains[0]
    my_jobs = lax.dynamic_index_in_dim(job_adapter, owner_index, 0, keepdims=False)
    my_blocks = lax.dynamic_slice_in_dim(
        block_adapter_ids, owner_index * local_blocks, local_blocks
    )
    slab_ids = jnp.arange(slab_count, dtype=jnp.int32)
    matching = (job_adapter[None, None] == my_blocks[:, None, None, None]) & (
        job_slab[None, None] == slab_ids[None, :, None, None]
    )
    owner_ids = jnp.arange(owner_total, dtype=jnp.int32)
    source_owner = jnp.sum(jnp.where(matching, owner_ids[None, None, :, None], 0), axis=(2, 3))
    own_select = (block_adapter_ids[:, None] == my_jobs[None, :]) & (my_jobs[None, :] >= 0)
    slot_rows = jnp.arange(local_blocks, dtype=jnp.int32)[:, None]

    def hand_out(owned):
        picked = jnp.dot(own_select.astype(jnp.bfloat16), owned, preferred_element_type=jnp.float32)
        return picked.astype(jnp.bfloat16).reshape(owner_total, local_blocks, panel_width)

    def assemble(arrived):
        gathered_slabs = arrived[source_owner, slot_rows]
        return gathered_slabs.reshape(local_blocks, slab_count * panel_width)

    gathered_panels = assemble(
        lax.all_to_all(
            hand_out(slot_adapter_params[0]), "dp", split_axis=0, concat_axis=0, tiled=True
        )
    )
    adapter_down_every = gathered_panels[:, :divide_position].reshape(
        local_blocks, hidden_width, ADAPTER_RANK
    )
    adapter_up_every = gathered_panels[:, divide_position:].reshape(
        local_blocks, ADAPTER_RANK, value_feature_width
    )
    micro_rows = MROWS
    micro_count = tok_dev // micro_rows
    per_block = block_rows // micro_rows
    step_count = section_total + micro_count - 1
    token_micro = tokens.reshape(micro_count, micro_rows, hidden_width)
    cot_micro = cotangent.reshape(micro_count, micro_rows, hidden_width)

    def forward_step(state_tuple, step_number):
        incoming, saved_in, saved_scale, saved_normed, saved_low = state_tuple
        micro_index = step_number - section_index
        is_valid = (micro_index >= 0) & (micro_index < micro_count)
        micro_slot = jnp.clip(micro_index, 0, micro_count - 1)
        hidden_state = jnp.where(section_index == 0, select_slot(token_micro, micro_slot), incoming)
        block_slot_index = micro_slot // per_block

        def forward_run_layer(unused):
            return layer_ahead_pass(
                hidden_state,
                gain_vector_row,
                value_complete,
                output_complete,
                select_slot(adapter_down_every, block_slot_index),
                select_slot(adapter_up_every, block_slot_index),
            )

        def forward_skip_layer(unused):
            return (
                jnp.zeros((micro_rows, hidden_width), jnp.bfloat16),
                jnp.zeros((micro_rows, 1), jnp.float32),
                jnp.zeros((micro_rows, hidden_width), jnp.bfloat16),
                jnp.zeros((micro_rows, ADAPTER_RANK), jnp.bfloat16),
            )

        output_block_rows, norm_gain_scale, normalized_rows, rank_projected = lax.cond(
            is_valid, forward_run_layer, forward_skip_layer, None
        )
        saved_in = put_slot(saved_in, hidden_state, micro_slot, is_valid)
        saved_scale = put_slot(saved_scale, norm_gain_scale, micro_slot, is_valid)
        saved_normed = put_slot(saved_normed, normalized_rows, micro_slot, is_valid)
        saved_low = put_slot(saved_low, rank_projected, micro_slot, is_valid)
        passed = from_behind(output_block_rows, "section", 1)
        return ((passed, saved_in, saved_scale, saved_normed, saved_low), None)

    forward_init = (
        jnp.zeros((micro_rows, hidden_width), jnp.bfloat16),
        jnp.zeros((micro_count, micro_rows, hidden_width), jnp.bfloat16),
        jnp.zeros((micro_count, micro_rows, 1), jnp.float32),
        jnp.zeros((micro_count, micro_rows, hidden_width), jnp.bfloat16),
        jnp.zeros((micro_count, micro_rows, ADAPTER_RANK), jnp.bfloat16),
    )
    forward_done, _ = lax.scan(forward_step, forward_init, jnp.arange(step_count, dtype=jnp.int32))
    _, saved_in, saved_scale, saved_normed, saved_low = forward_done

    def backward_step(state_tuple, step_number):
        incoming, block_grads = state_tuple
        micro_index = step_number - (section_total - 1 - section_index)
        is_valid = (micro_index >= 0) & (micro_index < micro_count)
        micro_slot = jnp.clip(micro_index, 0, micro_count - 1)
        output_gradient = jnp.where(
            section_index == section_total - 1, select_slot(cot_micro, micro_slot), incoming
        )
        block_slot_index = micro_slot // per_block

        def backward_run_layer(unused):
            return layer_reverse_pass(
                output_gradient,
                select_slot(saved_in, micro_slot),
                select_slot(saved_scale, micro_slot),
                select_slot(saved_normed, micro_slot),
                select_slot(saved_low, micro_slot),
                gain_vector_row,
                value_complete,
                output_complete,
                select_slot(adapter_down_every, block_slot_index),
                select_slot(adapter_up_every, block_slot_index),
            )

        def backward_skip_layer(unused):
            return (
                jnp.zeros((micro_rows, hidden_width), jnp.bfloat16),
                jnp.zeros((hidden_width, ADAPTER_RANK), jnp.float32),
                jnp.zeros((ADAPTER_RANK, value_feature_width), jnp.float32),
            )

        grad_in, down_gradient, up_gradient = lax.cond(
            is_valid, backward_run_layer, backward_skip_layer, None
        )
        grad_term = jnp.concatenate([down_gradient.reshape(-1), up_gradient.reshape(-1)])
        block_grads = block_grads.at[block_slot_index].add(jnp.where(is_valid, grad_term, 0.0))
        passed = from_behind(grad_in, "section", -1)
        return ((passed, block_grads), None)

    backward_init = (
        jnp.zeros((micro_rows, hidden_width), jnp.bfloat16),
        jnp.zeros((local_blocks, slab_count * panel_width), jnp.float32),
    )
    backward_done, _ = lax.scan(
        backward_step, backward_init, jnp.arange(step_count, dtype=jnp.int32)
    )
    block_grads = backward_done[1]
    outgoing = (
        jnp.zeros((owner_total, local_blocks, panel_width), jnp.float32)
        .at[source_owner, slot_rows]
        .set(block_grads.reshape(local_blocks, slab_count, panel_width))
    )
    arrived = lax.all_to_all(
        outgoing.astype(jnp.bfloat16), "dp", split_axis=0, concat_axis=0, tiled=True
    ).astype(outgoing.dtype)
    summed = jnp.dot(
        own_select.astype(jnp.float32).T,
        arrived.reshape(block_total, panel_width),
        precision=lax.Precision.HIGHEST,
        preferred_element_type=jnp.float32,
    )
    live = my_jobs >= 0
    adapter_ids = jnp.arange(adapter_total, dtype=jnp.int32)
    slot_counts = jnp.sum(
        jnp.where(adapter_ids[None, :] == my_jobs[:, None], token_counts[None, :], 0), axis=1
    )
    slot_counts = jnp.where(live, slot_counts, 1)
    slot_grad = summed / slot_counts.astype(jnp.float32)[:, None]
    params_new, first_new, second_new = adam_update(
        slot_adapter_params[0], first_moment[0], second_moment[0], slot_grad, live[:, None]
    )
    returned = assemble(
        lax.all_to_all(hand_out(params_new), "dp", split_axis=0, concat_axis=0, tiled=True)
    )
    return (params_new[None], first_new[None], second_new[None], returned[None])


def solution(mesh):
    return jax.shard_map(
        on_device,
        mesh=mesh,
        in_specs=(
            P("dp", None),
            P("dp", None),
            P("section", None),
            P("section", "dp", None),
            P("section", "dp", None),
            P(),
            P(),
            P(),
            P(),
            P("section", "dp", None),
            P("section", "dp", None),
            P("section", "dp", None),
        ),
        out_specs=(
            P("section", "dp", None),
            P("section", "dp", None),
            P("section", "dp", None),
            P("section", "dp", None),
        ),
        check_vma=False,
    )
```

profile of v0, /device:TPU:1, one launch (start us, length us, event | category | flops | bytes accessed | tf_op | source)
XLA Modules:
  0.0 1005.0 jit_solution(1554221455761827771)
XLA Ops:
  27.1 15.2 %all-to-all-done = bf16[32,2,4608]{2,1,0:T(2,128)(2,1)S(1)} async-done(((bf16[32,2,4608]{2,1,0:T(2,128)(2,1)}), bf16[32,2,4608]{2,1,0:T(2,128)(2,1)S(1)}, u32[]{:S(2)}, u32[]{:S(2)}) %all-to-all-start) | async-done | bytes 589856 | tf_op jit(solution)/shard_map/all_to_all | solution.py:174
  48.8 42.8 %all-gather.3.cloned.1.call-done = bf16[1,8192,1024]{2,1,0:T(8,128)(2,1)} async-done(((bf16[1,256,1024]{2,1,0:T(8,128)(2,1)}), bf16[1,8192,1024]{2,1,0:T(8,128)(2,1)}) %all-gather.3.cloned.1.call-update) | async-done | bytes 16777232 | tf_op jit(solution)/shard_map/all_gather | solution.py:146
  91.6 74.4 %all-gather.5.cloned.1.call-done = bf16[1,8192,1024]{2,1,0:T(8,128)(2,1)} async-done(((bf16[1,256,1024]{2,1,0:T(8,128)(2,1)}), bf16[1,8192,1024]{2,1,0:T(8,128)(2,1)}) %all-gather.5.cloned.1.call-update) | async-done | bytes 16777232 | tf_op jit(solution)/shard_map/all_gather | solution.py:147
  169.0 320.4 %while.36 = (s32[]{:T(128)}, bf16[16,8192]{1,0:T(8,128)(2,1)S(1)}, bf16[8,16,8192]{2,1,0:T(8,128)(2,1)}, f32[8,16,1]{1,2,0:T(1,128)S(1)}, bf16[8,16,8192]{2,1,0:...) while((s32[]{:T(128)}, bf16[16,8192]{1,0:T(8,128)(2,1)S(1)}, ...), condition=%wide.region_5.6_spmd, body=%wide.region_1.5_spmd.sunk | while | flops 543343104 | bytes 42153352 | solution.py:234
  173.0 19.6 %conditional.5 = (bf16[16,8192]{1,0:T(8,128)(2,1)S(1)}, f32[16,1]{0,1:T(1,128)S(1)}, bf16[16,8192]{1,0:T(8,128)(2,1)S(1)}, bf16[16,16]{1,0:T(8,128)(2,1)}) conditional(s32[]{:T(128)} %convert_element_type.134, () %tuple.117, (bf16[16,8192]{1,0:T(8,128)(2,1)S(1)}, f32[1,8192]{1,0:T(1,128)S(1)}, bf16[8192,1024]{1,0:T(8,128)(2,1)}, ...), branch_computations={%region_2.2_spmd, %region_3.4_spmd} | conditional | flops 542949632 | bytes 37946776 | solution.py:217
  182.3 10.3 %fusion = bf16[16,8192]{1,0:T(8,128)(2,1)S(1)} fusion(bf16[8192,1024]{1,0:T(8,128)(2,1)} %get-tuple-element.485, f32[16,1024]{1,0:T(8,128)S(1)} %fusion.58, bf16[16,16]{1,0:T(8,128)(2,1)} %convolution_convert_fusion, bf16[16,8192]{1,0:T(8,128)(2,1)S(1)} %get-tuple-element.480, bf16[1,16,1024]{2,1,0:T(8,128)(2,1)S(1)} %get-tuple-element.484), kind=kOutput, calls=%fused_computation.4 | convolution fusion | flops 269402112 | bytes 17400320 | tf_op jit(solution)/shard_map/while/body/eval_jaxpr/cond/branch_1_fun/dot_general | solution.py:25
  203.6 19.6 %conditional.5 = (bf16[16,8192]{1,0:T(8,128)(2,1)S(1)}, f32[16,1]{0,1:T(1,128)S(1)}, bf16[16,8192]{1,0:T(8,128)(2,1)S(1)}, bf16[16,16]{1,0:T(8,128)(2,1)}) conditional(s32[]{:T(128)} %convert_element_type.134, () %tuple.117, (bf16[16,8192]{1,0:T(8,128)(2,1)S(1)}, f32[1,8192]{1,0:T(1,128)S(1)}, bf16[8192,1024]{1,0:T(8,128)(2,1)}, ...), branch_computations={%region_2.2_spmd, %region_3.4_spmd} | conditional | flops 542949632 | bytes 37946776 | solution.py:217
  212.8 10.3 %fusion = bf16[16,8192]{1,0:T(8,128)(2,1)S(1)} fusion(bf16[8192,1024]{1,0:T(8,128)(2,1)} %get-tuple-element.485, f32[16,1024]{1,0:T(8,128)S(1)} %fusion.58, bf16[16,16]{1,0:T(8,128)(2,1)} %convolution_convert_fusion, bf16[16,8192]{1,0:T(8,128)(2,1)S(1)} %get-tuple-element.480, bf16[1,16,1024]{2,1,0:T(8,128)(2,1)S(1)} %get-tuple-element.484), kind=kOutput, calls=%fused_computation.4 | convolution fusion | flops 269402112 | bytes 17400320 | tf_op jit(solution)/shard_map/while/body/eval_jaxpr/cond/branch_1_fun/dot_general | solution.py:25
  236.0 19.6 %conditional.5 = (bf16[16,8192]{1,0:T(8,128)(2,1)S(1)}, f32[16,1]{0,1:T(1,128)S(1)}, bf16[16,8192]{1,0:T(8,128)(2,1)S(1)}, bf16[16,16]{1,0:T(8,128)(2,1)}) conditional(s32[]{:T(128)} %convert_element_type.134, () %tuple.117, (bf16[16,8192]{1,0:T(8,128)(2,1)S(1)}, f32[1,8192]{1,0:T(1,128)S(1)}, bf16[8192,1024]{1,0:T(8,128)(2,1)}, ...), branch_computations={%region_2.2_spmd, %region_3.4_spmd} | conditional | flops 542949632 | bytes 37946776 | solution.py:217
  245.3 10.3 %fusion = bf16[16,8192]{1,0:T(8,128)(2,1)S(1)} fusion(bf16[8192,1024]{1,0:T(8,128)(2,1)} %get-tuple-element.485, f32[16,1024]{1,0:T(8,128)S(1)} %fusion.58, bf16[16,16]{1,0:T(8,128)(2,1)} %convolution_convert_fusion, bf16[16,8192]{1,0:T(8,128)(2,1)S(1)} %get-tuple-element.480, bf16[1,16,1024]{2,1,0:T(8,128)(2,1)S(1)} %get-tuple-element.484), kind=kOutput, calls=%fused_computation.4 | convolution fusion | flops 269402112 | bytes 17400320 | tf_op jit(solution)/shard_map/while/body/eval_jaxpr/cond/branch_1_fun/dot_general | solution.py:25
  267.7 19.6 %conditional.5 = (bf16[16,8192]{1,0:T(8,128)(2,1)S(1)}, f32[16,1]{0,1:T(1,128)S(1)}, bf16[16,8192]{1,0:T(8,128)(2,1)S(1)}, bf16[16,16]{1,0:T(8,128)(2,1)}) conditional(s32[]{:T(128)} %convert_element_type.134, () %tuple.117, (bf16[16,8192]{1,0:T(8,128)(2,1)S(1)}, f32[1,8192]{1,0:T(1,128)S(1)}, bf16[8192,1024]{1,0:T(8,128)(2,1)}, ...), branch_computations={%region_2.2_spmd, %region_3.4_spmd} | conditional | flops 542949632 | bytes 37946776 | solution.py:217
  276.9 10.3 %fusion = bf16[16,8192]{1,0:T(8,128)(2,1)S(1)} fusion(bf16[8192,1024]{1,0:T(8,128)(2,1)} %get-tuple-element.485, f32[16,1024]{1,0:T(8,128)S(1)} %fusion.58, bf16[16,16]{1,0:T(8,128)(2,1)} %convolution_convert_fusion, bf16[16,8192]{1,0:T(8,128)(2,1)S(1)} %get-tuple-element.480, bf16[1,16,1024]{2,1,0:T(8,128)(2,1)S(1)} %get-tuple-element.484), kind=kOutput, calls=%fused_computation.4 | convolution fusion | flops 269402112 | bytes 17400320 | tf_op jit(solution)/shard_map/while/body/eval_jaxpr/cond/branch_1_fun/dot_general | solution.py:25
  298.6 19.6 %conditional.5 = (bf16[16,8192]{1,0:T(8,128)(2,1)S(1)}, f32[16,1]{0,1:T(1,128)S(1)}, bf16[16,8192]{1,0:T(8,128)(2,1)S(1)}, bf16[16,16]{1,0:T(8,128)(2,1)}) conditional(s32[]{:T(128)} %convert_element_type.134, () %tuple.117, (bf16[16,8192]{1,0:T(8,128)(2,1)S(1)}, f32[1,8192]{1,0:T(1,128)S(1)}, bf16[8192,1024]{1,0:T(8,128)(2,1)}, ...), branch_computations={%region_2.2_spmd, %region_3.4_spmd} | conditional | flops 542949632 | bytes 37946776 | solution.py:217
  307.9 10.3 %fusion = bf16[16,8192]{1,0:T(8,128)(2,1)S(1)} fusion(bf16[8192,1024]{1,0:T(8,128)(2,1)} %get-tuple-element.485, f32[16,1024]{1,0:T(8,128)S(1)} %fusion.58, bf16[16,16]{1,0:T(8,128)(2,1)} %convolution_convert_fusion, bf16[16,8192]{1,0:T(8,128)(2,1)S(1)} %get-tuple-element.480, bf16[1,16,1024]{2,1,0:T(8,128)(2,1)S(1)} %get-tuple-element.484), kind=kOutput, calls=%fused_computation.4 | convolution fusion | flops 269402112 | bytes 17400320 | tf_op jit(solution)/shard_map/while/body/eval_jaxpr/cond/branch_1_fun/dot_general | solution.py:25
  329.3 19.6 %conditional.5 = (bf16[16,8192]{1,0:T(8,128)(2,1)S(1)}, f32[16,1]{0,1:T(1,128)S(1)}, bf16[16,8192]{1,0:T(8,128)(2,1)S(1)}, bf16[16,16]{1,0:T(8,128)(2,1)}) conditional(s32[]{:T(128)} %convert_element_type.134, () %tuple.117, (bf16[16,8192]{1,0:T(8,128)(2,1)S(1)}, f32[1,8192]{1,0:T(1,128)S(1)}, bf16[8192,1024]{1,0:T(8,128)(2,1)}, ...), branch_computations={%region_2.2_spmd, %region_3.4_spmd} | conditional | flops 542949632 | bytes 37946776 | solution.py:217
  360.0 19.6 %conditional.5 = (bf16[16,8192]{1,0:T(8,128)(2,1)S(1)}, f32[16,1]{0,1:T(1,128)S(1)}, bf16[16,8192]{1,0:T(8,128)(2,1)S(1)}, bf16[16,16]{1,0:T(8,128)(2,1)}) conditional(s32[]{:T(128)} %convert_element_type.134, () %tuple.117, (bf16[16,8192]{1,0:T(8,128)(2,1)S(1)}, f32[1,8192]{1,0:T(1,128)S(1)}, bf16[8192,1024]{1,0:T(8,128)(2,1)}, ...), branch_computations={%region_2.2_spmd, %region_3.4_spmd} | conditional | flops 542949632 | bytes 37946776 | solution.py:217
  390.7 19.6 %conditional.5 = (bf16[16,8192]{1,0:T(8,128)(2,1)S(1)}, f32[16,1]{0,1:T(1,128)S(1)}, bf16[16,8192]{1,0:T(8,128)(2,1)S(1)}, bf16[16,16]{1,0:T(8,128)(2,1)}) conditional(s32[]{:T(128)} %convert_element_type.134, () %tuple.117, (bf16[16,8192]{1,0:T(8,128)(2,1)S(1)}, f32[1,8192]{1,0:T(1,128)S(1)}, bf16[8192,1024]{1,0:T(8,128)(2,1)}, ...), branch_computations={%region_2.2_spmd, %region_3.4_spmd} | conditional | flops 542949632 | bytes 37946776 | solution.py:217
  422.0 22.7 %collective-permute-start = (bf16[16,8192]{1,0:T(8,128)(2,1)S(1)}, bf16[16,8192]{1,0:T(8,128)(2,1)S(1)}, u32[]{:S(2)}, u32[]{:S(2)}) collective-permute-start(bf16[16,8192]{1,0:T(8,128)(2,1)S(1)} %get-tuple-element.992), channel_id=1, source_target_pairs={{0,32},{32,64},{64,96},{1,33},{33,65},{65,97},{2,34},{34,66},{66,9... | collective-permute-start | bytes 786440 | tf_op jit(solution)/shard_map/while/body/eval_jaxpr/ppermute | solution.py:21
  464.4 21.8 %collective-permute-start = (bf16[16,8192]{1,0:T(8,128)(2,1)S(1)}, bf16[16,8192]{1,0:T(8,128)(2,1)S(1)}, u32[]{:S(2)}, u32[]{:S(2)}) collective-permute-start(bf16[16,8192]{1,0:T(8,128)(2,1)S(1)} %get-tuple-element.992), channel_id=1, source_target_pairs={{0,32},{32,64},{64,96},{1,33},{33,65},{65,97},{2,34},{34,66},{66,9... | collective-permute-start | bytes 786440 | tf_op jit(solution)/shard_map/while/body/eval_jaxpr/ppermute | solution.py:21
  489.5 427.0 %while.37 = (s32[]{:T(128)}, bf16[16,8192]{1,0:T(8,128)(2,1)S(1)}, f32[1,147456]{1,0:T(1,128)S(1)}, s32[11]{0:T(128)S(1)}, s32[]{:T(128)}, /*index=5*/pred[]{:T(...) while((s32[]{:T(128)}, bf16[16,8192]{1,0:T(8,128)(2,1)S(1)}, ...), condition=%wide.region_11.12_spmd.clone, body=%wide.region_6.11_spmd.clone.sunk | while | flops 549044800 | bytes 42802872 | solution.py:280
  506.0 19.6 %collective-permute-done.1 = bf16[16,8192]{1,0:T(8,128)(2,1)S(1)} collective-permute-done((bf16[16,8192]{1,0:T(8,128)(2,1)S(1)}, bf16[16,8192]{1,0:T(8,128)(2,1)S(1)}, u32[]{:S(2)}, u32[]{:S(2)}) %collective-permute-start.1) | collective-permute-done | bytes 262176 | tf_op jit(solution)/shard_map/while/body/eval_jaxpr/ppermute | solution.py:21
  532.4 87.0 %collective-permute-done.1 = bf16[16,8192]{1,0:T(8,128)(2,1)S(1)} collective-permute-done((bf16[16,8192]{1,0:T(8,128)(2,1)S(1)}, bf16[16,8192]{1,0:T(8,128)(2,1)S(1)}, u32[]{:S(2)}, u32[]{:S(2)}) %collective-permute-start.1) | collective-permute-done | bytes 262176 | tf_op jit(solution)/shard_map/while/body/eval_jaxpr/ppermute | solution.py:21
  620.7 28.8 %conditional.6 = (bf16[16,8192]{1,0:T(8,128)(2,1)S(1)}, f32[1,131072]{1,0:T(1,128)S(1)}, f32[1,16384]{1,0:T(1,128)S(1)}) conditional(s32[]{:T(128)} %convert_element_type.135, () %tuple.120, (pred[]{:T(512)}, bf16[8,16,8192]{2,1,0:T(8,128)(2,1)}, s32[]{:T(128)}, bf16[16,8192]{1,0:T(8,128)(2,1)S(1)}, f32[8,16,1]{1,2,0:T(1,128)S(1)}, ...), branch_computations={%region_7.7_spmd, %region_8.9_spmd} | conditional | flops 548307520 | bytes 39984272 | solution.py:268
  657.8 28.8 %conditional.6 = (bf16[16,8192]{1,0:T(8,128)(2,1)S(1)}, f32[1,131072]{1,0:T(1,128)S(1)}, f32[1,16384]{1,0:T(1,128)S(1)}) conditional(s32[]{:T(128)} %convert_element_type.135, () %tuple.120, (pred[]{:T(512)}, bf16[8,16,8192]{2,1,0:T(8,128)(2,1)}, s32[]{:T(128)}, bf16[16,8192]{1,0:T(8,128)(2,1)S(1)}, f32[8,16,1]{1,2,0:T(1,128)S(1)}, ...), branch_computations={%region_7.7_spmd, %region_8.9_spmd} | conditional | flops 548307520 | bytes 39984272 | solution.py:268
  694.9 28.8 %conditional.6 = (bf16[16,8192]{1,0:T(8,128)(2,1)S(1)}, f32[1,131072]{1,0:T(1,128)S(1)}, f32[1,16384]{1,0:T(1,128)S(1)}) conditional(s32[]{:T(128)} %convert_element_type.135, () %tuple.120, (pred[]{:T(512)}, bf16[8,16,8192]{2,1,0:T(8,128)(2,1)}, s32[]{:T(128)}, bf16[16,8192]{1,0:T(8,128)(2,1)S(1)}, f32[8,16,1]{1,2,0:T(1,128)S(1)}, ...), branch_computations={%region_7.7_spmd, %region_8.9_spmd} | conditional | flops 548307520 | bytes 39984272 | solution.py:268
  732.1 28.8 %conditional.6 = (bf16[16,8192]{1,0:T(8,128)(2,1)S(1)}, f32[1,131072]{1,0:T(1,128)S(1)}, f32[1,16384]{1,0:T(1,128)S(1)}) conditional(s32[]{:T(128)} %convert_element_type.135, () %tuple.120, (pred[]{:T(512)}, bf16[8,16,8192]{2,1,0:T(8,128)(2,1)}, s32[]{:T(128)}, bf16[16,8192]{1,0:T(8,128)(2,1)S(1)}, f32[8,16,1]{1,2,0:T(1,128)S(1)}, ...), branch_computations={%region_7.7_spmd, %region_8.9_spmd} | conditional | flops 548307520 | bytes 39984272 | solution.py:268
  769.2 28.8 %conditional.6 = (bf16[16,8192]{1,0:T(8,128)(2,1)S(1)}, f32[1,131072]{1,0:T(1,128)S(1)}, f32[1,16384]{1,0:T(1,128)S(1)}) conditional(s32[]{:T(128)} %convert_element_type.135, () %tuple.120, (pred[]{:T(512)}, bf16[8,16,8192]{2,1,0:T(8,128)(2,1)}, s32[]{:T(128)}, bf16[16,8192]{1,0:T(8,128)(2,1)S(1)}, f32[8,16,1]{1,2,0:T(1,128)S(1)}, ...), branch_computations={%region_7.7_spmd, %region_8.9_spmd} | conditional | flops 548307520 | bytes 39984272 | solution.py:268
  806.4 28.8 %conditional.6 = (bf16[16,8192]{1,0:T(8,128)(2,1)S(1)}, f32[1,131072]{1,0:T(1,128)S(1)}, f32[1,16384]{1,0:T(1,128)S(1)}) conditional(s32[]{:T(128)} %convert_element_type.135, () %tuple.120, (pred[]{:T(512)}, bf16[8,16,8192]{2,1,0:T(8,128)(2,1)}, s32[]{:T(128)}, bf16[16,8192]{1,0:T(8,128)(2,1)S(1)}, f32[8,16,1]{1,2,0:T(1,128)S(1)}, ...), branch_computations={%region_7.7_spmd, %region_8.9_spmd} | conditional | flops 548307520 | bytes 39984272 | solution.py:268
  843.5 28.8 %conditional.6 = (bf16[16,8192]{1,0:T(8,128)(2,1)S(1)}, f32[1,131072]{1,0:T(1,128)S(1)}, f32[1,16384]{1,0:T(1,128)S(1)}) conditional(s32[]{:T(128)} %convert_element_type.135, () %tuple.120, (pred[]{:T(512)}, bf16[8,16,8192]{2,1,0:T(8,128)(2,1)}, s32[]{:T(128)}, bf16[16,8192]{1,0:T(8,128)(2,1)S(1)}, f32[8,16,1]{1,2,0:T(1,128)S(1)}, ...), branch_computations={%region_7.7_spmd, %region_8.9_spmd} | conditional | flops 548307520 | bytes 39984272 | solution.py:268
  880.6 28.8 %conditional.6 = (bf16[16,8192]{1,0:T(8,128)(2,1)S(1)}, f32[1,131072]{1,0:T(1,128)S(1)}, f32[1,16384]{1,0:T(1,128)S(1)}) conditional(s32[]{:T(128)} %convert_element_type.135, () %tuple.120, (pred[]{:T(512)}, bf16[8,16,8192]{2,1,0:T(8,128)(2,1)}, s32[]{:T(128)}, bf16[16,8192]{1,0:T(8,128)(2,1)S(1)}, f32[8,16,1]{1,2,0:T(1,128)S(1)}, ...), branch_computations={%region_7.7_spmd, %region_8.9_spmd} | conditional | flops 548307520 | bytes 39984272 | solution.py:268
  926.7 28.0 %all-to-all-start.1 = ((bf16[32,2,4608]{2,1,0:T(2,128)(2,1)}), bf16[32,2,4608]{2,1,0:T(2,128)(2,1)S(1)}, u32[]{:S(2)}, u32[]{:S(2)}) async-start(bf16[32,2,4608]{2,1,0:T(2,128)(2,1)} %reshape.278), calls=%async_computation.1 | async-start | bytes 1179648 | tf_op jit(solution)/shard_map/all_to_all | solution.py:289
  954.9 12.0 %all-to-all-done.1 = bf16[32,2,4608]{2,1,0:T(2,128)(2,1)S(1)} async-done(((bf16[32,2,4608]{2,1,0:T(2,128)(2,1)}), bf16[32,2,4608]{2,1,0:T(2,128)(2,1)S(1)}, u32[]{:S(2)}, u32[]{:S(2)}) %all-to-all-start.1) | async-done | bytes 589856 | tf_op jit(solution)/shard_map/all_to_all | solution.py:289
  (440 shorter events, 601.7 us)
Async XLA Ops:
  7.2 84.4 %all-gather.3.cloned.1.call-start = ((), (), s32[]{:S(2)}) async-start(), calls=%async_computation.3 | async-start | bytes 17301504 | tf_op jit(solution)/shard_map/all_gather | solution.py:146
  7.9 158.0 %all-gather.5.cloned.1.call-start = ((), (), s32[]{:S(2)}) async-start(), calls=%async_computation.4 | async-start | bytes 17301504 | tf_op jit(solution)/shard_map/all_gather | solution.py:147
  15.3 27.1 %all-to-all-start = ((bf16[32,2,4608]{2,1,0:T(2,128)(2,1)}), bf16[32,2,4608]{2,1,0:T(2,128)(2,1)S(1)}, u32[]{:S(2)}, u32[]{:S(2)}) async-start(bf16[32,2,4608]{2,1,0:T(2,128)(2,1)} %reshape.276), calls=%async_computation | async-start | bytes 1179648 | tf_op jit(solution)/shard_map/all_to_all | solution.py:174
  48.6 120.4 %copy-start.2 = (f32[1,8192]{1,0:T(1,128)S(1)}, f32[1,8192]{1,0:T(1,128)}, u32[]{:S(2)}) copy-start(f32[1,8192]{1,0:T(1,128)} %param.24) | copy-start | bytes 98308
  192.6 7.0 collective-permute-start
  223.1 8.9 collective-permute-start
  255.6 8.1 collective-permute-start
  287.2 7.4 collective-permute-start
  318.2 7.1 collective-permute-start
  348.9 7.1 collective-permute-start
  379.5 7.1 collective-permute-start
  410.2 7.1 collective-permute-start
  422.0 26.0 %collective-permute-start = (bf16[16,8192]{1,0:T(8,128)(2,1)S(1)}, bf16[16,8192]{1,0:T(8,128)(2,1)S(1)}, u32[]{:S(2)}, u32[]{:S(2)}) collective-permute-start(bf16[16,8192]{1,0:T(8,128)(2,1)S(1)} %get-tuple-element.992), channel_id=1, source_target_pairs={{0,32},{32,64},{64,96},{1,33},{33,65},{65,97},{2,34},{34,66},{66,9... | collective-permute-start | bytes 786440 | tf_op jit(solution)/shard_map/while/body/eval_jaxpr/ppermute | solution.py:21
  452.7 7.1 collective-permute-start
  464.4 25.1 %collective-permute-start = (bf16[16,8192]{1,0:T(8,128)(2,1)S(1)}, bf16[16,8192]{1,0:T(8,128)(2,1)S(1)}, u32[]{:S(2)}, u32[]{:S(2)}) collective-permute-start(bf16[16,8192]{1,0:T(8,128)(2,1)S(1)} %get-tuple-element.992), channel_id=1, source_target_pairs={{0,32},{32,64},{64,96},{1,33},{33,65},{65,97},{2,34},{34,66},{66,9... | collective-permute-start | bytes 786440 | tf_op jit(solution)/shard_map/while/body/eval_jaxpr/ppermute | solution.py:21
  491.3 8.0 collective-permute-start.1
  500.9 24.8 %collective-permute-start.1 = (bf16[16,8192]{1,0:T(8,128)(2,1)S(1)}, bf16[16,8192]{1,0:T(8,128)(2,1)S(1)}, u32[]{:S(2)}, u32[]{:S(2)}) collective-permute-start(bf16[16,8192]{1,0:T(8,128)(2,1)S(1)} %get-tuple-element.1013), channel_id=1, source_target_pairs={{32,0},{64,32},{96,64},{33,1},{65,33},{97,65},{34,2},{66,34},{98,6... | collective-permute-start | bytes 786440 | tf_op jit(solution)/shard_map/while/body/eval_jaxpr/ppermute | solution.py:21
  527.3 92.2 %collective-permute-start.1 = (bf16[16,8192]{1,0:T(8,128)(2,1)S(1)}, bf16[16,8192]{1,0:T(8,128)(2,1)S(1)}, u32[]{:S(2)}, u32[]{:S(2)}) collective-permute-start(bf16[16,8192]{1,0:T(8,128)(2,1)S(1)} %get-tuple-element.1013), channel_id=1, source_target_pairs={{32,0},{64,32},{96,64},{33,1},{65,33},{97,65},{34,2},{66,34},{98,6... | collective-permute-start | bytes 786440 | tf_op jit(solution)/shard_map/while/body/eval_jaxpr/ppermute | solution.py:21
  649.4 7.1 collective-permute-start.1
  686.6 7.1 collective-permute-start.1
  723.7 7.1 collective-permute-start.1
  760.9 7.1 collective-permute-start.1
  798.0 7.1 collective-permute-start.1
  835.1 7.1 collective-permute-start.1
  872.3 7.1 collective-permute-start.1
  909.4 7.1 collective-permute-start.1
  925.4 43.3 %copy-start.12 = (s32[32]{0:T(128)S(1)}, s32[32]{0:T(128)}, u32[]{:S(2)}) copy-start(s32[32]{0:T(128)} %param.27) | copy-start | bytes 388
  925.4 43.3 %copy-start.14 = (pred[64]{0:T(512)(128)(4,1)S(1)}, pred[64]{0:T(512)(128)(4,1)}, u32[]{:S(2)}) copy-start(pred[64]{0:T(512)(128)(4,1)} %copy-done.13) | copy-start | bytes 196
  925.4 43.3 %copy-start.15 = (pred[64]{0:T(512)(128)(4,1)S(1)}, pred[64]{0:T(512)(128)(4,1)}, u32[]{:S(2)}) copy-start(pred[64]{0:T(512)(128)(4,1)} %get-tuple-element.797) | copy-start | bytes 196
  926.7 42.0 %copy-start.3 = (f32[1,64,9216]{2,1,0:T(8,128)S(1)}, f32[1,64,9216]{2,1,0:T(8,128)}, u32[]{:S(2)}) copy-start(f32[1,64,9216]{2,1,0:T(8,128)} %param.33) | copy-start | bytes 7077892
  926.7 40.3 %all-to-all-start.1 = ((bf16[32,2,4608]{2,1,0:T(2,128)(2,1)}), bf16[32,2,4608]{2,1,0:T(2,128)(2,1)S(1)}, u32[]{:S(2)}, u32[]{:S(2)}) async-start(bf16[32,2,4608]{2,1,0:T(2,128)(2,1)} %reshape.278), calls=%async_computation.1 | async-start | bytes 1179648 | tf_op jit(solution)/shard_map/all_to_all | solution.py:289
  978.7 15.9 %all-to-all-start.2 = ((bf16[32,2,4608]{2,1,0:T(2,128)(2,1)}), bf16[32,2,4608]{2,1,0:T(2,128)(2,1)S(1)}, u32[]{:S(2)}, u32[]{:S(2)}) async-start(bf16[32,2,4608]{2,1,0:T(2,128)(2,1)} %reshape.280), calls=%async_computation.2 | async-start | bytes 1179648 | tf_op jit(solution)/shard_map/all_to_all | solution.py:309
  (26 other events, 295.1 us)
Sparse Core Ops, SparseCore 0:
  10.2 81.2 all-gather.2
  93.8 72.0 all-gather.4
where the time goes:
time: 1020 us; the launch traced here: 1010 us
  matrix products  352 us (35%)
  waiting for transfers between devices  293 us (29%)
  starting transfers between devices  133 us (13%)
  other arithmetic  107 us (10%)
  local copies, waits for them, and re-layouts  89.5 us (9%)
  loops' own time  16.4 us (2%)
  between operations  14.8 us (1%)
    dot_general x32, matrix products, contract_trailing(): lax.dot_general(left, right, (((1,), (1,)), ((), ())), preferred_element_...  176 us
    ppermute x22, waiting for transfers between devices, from_behind(): return lax.ppermute(shard, axis, pairs)  141 us
    ppermute x22, starting transfers between devices, from_behind(): return lax.ppermute(shard, axis, pairs)  91.5 us
    all_gather x1, waiting for transfers between devices, on_device(): lax.all_gather(output_projection_weight, 'dp', axis=1, tiled=True)  74.4 us
    dot_general x8, matrix products, layer_reverse_pass(): jnp.dot(output_gradient, output_complete, preferred_element_type=jnp.floa...  65.1 us
    dot_general x8, matrix products, layer_ahead_pass(): jnp.dot(normalized_rows, value_complete, preferred_element_type=jnp.float32)  64.4 us
    all_gather x1, waiting for transfers between devices, on_device(): lax.all_gather(value_projection_weight, 'dp', axis=1, tiled=True)  42.8 us
    scatter-add x11, other arithmetic, backward_step(): block_grads.at[block_slot_index].add(jnp.where(is_valid, grad_term, 0.0))  33.9 us
  transfers between devices with their start and end apart: 27, of which 27 were waited for; matrix products, arithmetic and copies ran while one was open for 9% of the time, Pallas kernels for 0%

commit v1 on v0

--- a/solution.py
+++ b/solution.py
@@ -13,6 +13,11 @@
 FIRST_FIX = 1.0 - 0.9**50 * 0.9**50
 SECOND_FIX = 1.0 - 0.999**50 * 0.999**50
 NORM_EPS = 1e-05
+
+
+def swapped_in(x, axis, d):
+    sent = jnp.stack([x] * lax.axis_size(axis))
+    return jnp.concatenate(lax.all_to_all(sent, axis, 0, 0), axis=d)
 
 
 def from_behind(shard, axis, by):
@@ -144,7 +149,7 @@
     divide_position = hidden_width * ADAPTER_RANK
     value_complete, output_complete = (
         lax.all_gather(value_projection_weight, "dp", axis=1, tiled=True),
-        lax.all_gather(output_projection_weight, "dp", axis=1, tiled=True),
+        swapped_in(output_projection_weight, "dp", 1),
     )
     value_complete = value_complete[0]
     output_complete = output_complete[0]

time: 1020 us -> 1170 us (1.15); the launches traced: 1010 us -> 1170 us
  waiting for transfers between devices: 293 us -> 376 us
  starting transfers between devices: 133 us -> 180 us
  blocking collectives: 0 us -> 26.5 us
    all_to_all x1, waiting for transfers between devices: 15.2 us -> 222 us  [swapped_in(): return jnp.concatenate(lax.all_to_all(sent, axis, 0, 0), axis=d)]
    all_gather x1 -> x0, waiting for transfers between devices: 74.4 us -> none  [on_device(): lax.all_gather(output_projection_weight, 'dp', axis=1, tiled=True)]
    all_to_all x1, starting transfers between devices: 28 us -> 81.4 us  [on_device(): lax.all_to_all(outgoing.astype(jnp.bfloat16), 'dp', split_axis=0, concat_...]
    all_gather x1, waiting for transfers between devices: 42.8 us -> 0.01 us  [on_device(): lax.all_gather(value_projection_weight, 'dp', axis=1, tiled=True)]
    all_to_all x0 -> x1, blocking collectives: none -> 26.5 us  [on_device(): lax.all_to_all(hand_out(slot_adapter_params[0]), 'dp', split_axis=0, conc...]
  transfers between devices with their start and end apart: 27 -> 26, of which waited for: 27 -> 25; matrix products, arithmetic and copies ran while one was open for 9% -> 8% of each run, Pallas kernels for 0% -> 0%
where the time goes in v1:
time: 1170 us
  waiting for transfers between devices  376 us (32%)
  matrix products  352 us (30%)
  starting transfers between devices  180 us (15%)
  other arithmetic  106 us (9%)
  local copies, waits for them, and re-layouts  94.6 us (8%)
  blocking collectives  26.5 us (2%)
  loops' own time  16.4 us (1%)
  between operations  14.6 us (1%)
    all_to_all x1, waiting for transfers between devices, swapped_in(): return jnp.concatenate(lax.all_to_all(sent, axis, 0, 0), axis=d)  222 us
    dot_general x32, matrix products, contract_trailing(): lax.dot_general(left, right, (((1,), (1,)), ((), ())), preferred_element_...  176 us
    ppermute x22, waiting for transfers between devices, from_behind(): return lax.ppermute(shard, axis, pairs)  136 us
    ppermute x22, starting transfers between devices, from_behind(): return lax.ppermute(shard, axis, pairs)  89.7 us
    all_to_all x1, starting transfers between devices, on_device(): lax.all_to_all(outgoing.astype(jnp.bfloat16), 'dp', split_axis=0, concat_...  81.4 us
    dot_general x8, matrix products, layer_reverse_pass(): jnp.dot(output_gradient, output_complete, preferred_element_type=jnp.floa...  65.1 us
    dot_general x8, matrix products, layer_ahead_pass(): jnp.dot(normalized_rows, value_complete, preferred_element_type=jnp.float32)  64.4 us
    scatter-add x11, other arithmetic, backward_step(): block_grads.at[block_slot_index].add(jnp.where(is_valid, grad_term, 0.0))  33.9 us
  transfers between devices with their start and end apart: 26, of which 25 were waited for; matrix products, arithmetic and copies ran while one was open for 8% of the time, Pallas kernels for 0%

profile of v1, /device:TPU:1, one launch (start us, length us, event | category | flops | bytes accessed | tf_op | source)
XLA Modules:
  0.0 1167.1 jit_solution(436314627104125852)
XLA Ops:
  13.4 26.5 %all_to_all.20 = bf16[32,2,4608]{2,1,0:T(2,128)(2,1)S(1)} all-to-all(bf16[32,2,4608]{2,1,0:T(2,128)(2,1)S(1)} %reshape.279), channel_id=1, replica_groups=mesh['section'=4,'dp'=32] {'dp'}, dimensions={0} | all-to-all | bytes 1179648 | tf_op jit(solution)/shard_map/all_to_all | solution.py:179
  60.2 221.7 %all-to-all-done.1 = bf16[32,1,256,1024]{3,2,1,0:T(8,128)(2,1)} async-done(((bf16[32,1,256,1024]{3,2,1,0:T(8,128)(2,1)}), bf16[32,1,256,1024]{3,2,1,0:T(8,128)(2,1)}, u32[]{:S(2)}, u32[]{:S(2)}) %all-to-all-start.1) | async-done | bytes 16777248 | tf_op jit(solution)/shard_map/all_to_all | solution.py:20
  284.9 314.1 %while.36 = (s32[]{:T(128)}, bf16[16,8192]{1,0:T(8,128)(2,1)S(1)}, bf16[8,16,8192]{2,1,0:T(8,128)(2,1)}, f32[8,16,1]{1,2,0:T(1,128)S(1)}, bf16[8,16,8192]{2,1,0:...) while((s32[]{:T(128)}, bf16[16,8192]{1,0:T(8,128)(2,1)S(1)}, ...), condition=%wide.region_5.6_spmd, body=%wide.region_1.5_spmd.sunk | while | flops 543343104 | bytes 42153352 | solution.py:239
  288.9 19.6 %conditional.5 = (bf16[16,8192]{1,0:T(8,128)(2,1)S(1)}, f32[16,1]{0,1:T(1,128)S(1)}, bf16[16,8192]{1,0:T(8,128)(2,1)S(1)}, bf16[16,16]{1,0:T(8,128)(2,1)}) conditional(s32[]{:T(128)} %convert_element_type.134, () %tuple.117, (bf16[16,8192]{1,0:T(8,128)(2,1)S(1)}, f32[1,8192]{1,0:T(1,128)S(1)}, bf16[8192,1024]{1,0:T(8,128)(2,1)}, ...), branch_computations={%region_2.2_spmd, %region_3.4_spmd} | conditional | flops 542949632 | bytes 37946776 | solution.py:222
  298.2 10.3 fusion
  317.1 19.6 %conditional.5 = (bf16[16,8192]{1,0:T(8,128)(2,1)S(1)}, f32[16,1]{0,1:T(1,128)S(1)}, bf16[16,8192]{1,0:T(8,128)(2,1)S(1)}, bf16[16,16]{1,0:T(8,128)(2,1)}) conditional(s32[]{:T(128)} %convert_element_type.134, () %tuple.117, (bf16[16,8192]{1,0:T(8,128)(2,1)S(1)}, f32[1,8192]{1,0:T(1,128)S(1)}, bf16[8192,1024]{1,0:T(8,128)(2,1)}, ...), branch_computations={%region_2.2_spmd, %region_3.4_spmd} | conditional | flops 542949632 | bytes 37946776 | solution.py:222
  326.3 10.3 fusion
  347.8 19.6 %conditional.5 = (bf16[16,8192]{1,0:T(8,128)(2,1)S(1)}, f32[16,1]{0,1:T(1,128)S(1)}, bf16[16,8192]{1,0:T(8,128)(2,1)S(1)}, bf16[16,16]{1,0:T(8,128)(2,1)}) conditional(s32[]{:T(128)} %convert_element_type.134, () %tuple.117, (bf16[16,8192]{1,0:T(8,128)(2,1)S(1)}, f32[1,8192]{1,0:T(1,128)S(1)}, bf16[8192,1024]{1,0:T(8,128)(2,1)}, ...), branch_computations={%region_2.2_spmd, %region_3.4_spmd} | conditional | flops 542949632 | bytes 37946776 | solution.py:222
  357.0 10.3 fusion
  378.4 19.6 %conditional.5 = (bf16[16,8192]{1,0:T(8,128)(2,1)S(1)}, f32[16,1]{0,1:T(1,128)S(1)}, bf16[16,8192]{1,0:T(8,128)(2,1)S(1)}, bf16[16,16]{1,0:T(8,128)(2,1)}) conditional(s32[]{:T(128)} %convert_element_type.134, () %tuple.117, (bf16[16,8192]{1,0:T(8,128)(2,1)S(1)}, f32[1,8192]{1,0:T(1,128)S(1)}, bf16[8192,1024]{1,0:T(8,128)(2,1)}, ...), branch_computations={%region_2.2_spmd, %region_3.4_spmd} | conditional | flops 542949632 | bytes 37946776 | solution.py:222
  387.7 10.3 fusion
  409.1 19.6 %conditional.5 = (bf16[16,8192]{1,0:T(8,128)(2,1)S(1)}, f32[16,1]{0,1:T(1,128)S(1)}, bf16[16,8192]{1,0:T(8,128)(2,1)S(1)}, bf16[16,16]{1,0:T(8,128)(2,1)}) conditional(s32[]{:T(128)} %convert_element_type.134, () %tuple.117, (bf16[16,8192]{1,0:T(8,128)(2,1)S(1)}, f32[1,8192]{1,0:T(1,128)S(1)}, bf16[8192,1024]{1,0:T(8,128)(2,1)}, ...), branch_computations={%region_2.2_spmd, %region_3.4_spmd} | conditional | flops 542949632 | bytes 37946776 | solution.py:222
  418.3 10.3 fusion
  439.8 19.6 %conditional.5 = (bf16[16,8192]{1,0:T(8,128)(2,1)S(1)}, f32[16,1]{0,1:T(1,128)S(1)}, bf16[16,8192]{1,0:T(8,128)(2,1)S(1)}, bf16[16,16]{1,0:T(8,128)(2,1)}) conditional(s32[]{:T(128)} %convert_element_type.134, () %tuple.117, (bf16[16,8192]{1,0:T(8,128)(2,1)S(1)}, f32[1,8192]{1,0:T(1,128)S(1)}, bf16[8192,1024]{1,0:T(8,128)(2,1)}, ...), branch_computations={%region_2.2_spmd, %region_3.4_spmd} | conditional | flops 542949632 | bytes 37946776 | solution.py:222
  449.0 10.3 fusion
  470.5 19.6 %conditional.5 = (bf16[16,8192]{1,0:T(8,128)(2,1)S(1)}, f32[16,1]{0,1:T(1,128)S(1)}, bf16[16,8192]{1,0:T(8,128)(2,1)S(1)}, bf16[16,16]{1,0:T(8,128)(2,1)}) conditional(s32[]{:T(128)} %convert_element_type.134, () %tuple.117, (bf16[16,8192]{1,0:T(8,128)(2,1)S(1)}, f32[1,8192]{1,0:T(1,128)S(1)}, bf16[8192,1024]{1,0:T(8,128)(2,1)}, ...), branch_computations={%region_2.2_spmd, %region_3.4_spmd} | conditional | flops 542949632 | bytes 37946776 | solution.py:222
  501.1 19.6 %conditional.5 = (bf16[16,8192]{1,0:T(8,128)(2,1)S(1)}, f32[16,1]{0,1:T(1,128)S(1)}, bf16[16,8192]{1,0:T(8,128)(2,1)S(1)}, bf16[16,16]{1,0:T(8,128)(2,1)}) conditional(s32[]{:T(128)} %convert_element_type.134, () %tuple.117, (bf16[16,8192]{1,0:T(8,128)(2,1)S(1)}, f32[1,8192]{1,0:T(1,128)S(1)}, bf16[8192,1024]{1,0:T(8,128)(2,1)}, ...), branch_computations={%region_2.2_spmd, %region_3.4_spmd} | conditional | flops 542949632 | bytes 37946776 | solution.py:222
  532.5 22.8 %collective-permute-start = (bf16[16,8192]{1,0:T(8,128)(2,1)S(1)}, bf16[16,8192]{1,0:T(8,128)(2,1)S(1)}, u32[]{:S(2)}, u32[]{:S(2)}) collective-permute-start(bf16[16,8192]{1,0:T(8,128)(2,1)S(1)} %get-tuple-element.992), channel_id=1, source_target_pairs={{0,32},{32,64},{64,96},{1,33},{33,65},{65,97},{2,34},{34,66},{66,9... | collective-permute-start | bytes 786440 | tf_op jit(solution)/shard_map/while/body/eval_jaxpr/ppermute | solution.py:26
  574.9 20.9 %collective-permute-start = (bf16[16,8192]{1,0:T(8,128)(2,1)S(1)}, bf16[16,8192]{1,0:T(8,128)(2,1)S(1)}, u32[]{:S(2)}, u32[]{:S(2)}) collective-permute-start(bf16[16,8192]{1,0:T(8,128)(2,1)S(1)} %get-tuple-element.992), channel_id=1, source_target_pairs={{0,32},{32,64},{64,96},{1,33},{33,65},{65,97},{2,34},{34,66},{66,9... | collective-permute-start | bytes 786440 | tf_op jit(solution)/shard_map/while/body/eval_jaxpr/ppermute | solution.py:26
  599.1 426.6 %while.37 = (s32[]{:T(128)}, bf16[16,8192]{1,0:T(8,128)(2,1)S(1)}, f32[1,147456]{1,0:T(1,128)S(1)}, s32[11]{0:T(128)S(1)}, s32[]{:T(128)}, /*index=5*/pred[]{:T(...) while((s32[]{:T(128)}, bf16[16,8192]{1,0:T(8,128)(2,1)S(1)}, ...), condition=%wide.region_11.12_spmd.clone, body=%wide.region_6.11_spmd.clone.sunk | while | flops 549044800 | bytes 42802872 | solution.py:285
  615.2 19.7 %collective-permute-done.1 = bf16[16,8192]{1,0:T(8,128)(2,1)S(1)} collective-permute-done((bf16[16,8192]{1,0:T(8,128)(2,1)S(1)}, bf16[16,8192]{1,0:T(8,128)(2,1)S(1)}, u32[]{:S(2)}, u32[]{:S(2)}) %collective-permute-start.1) | collective-permute-done | bytes 262176 | tf_op jit(solution)/shard_map/while/body/eval_jaxpr/ppermute | solution.py:26
  641.6 86.8 %collective-permute-done.1 = bf16[16,8192]{1,0:T(8,128)(2,1)S(1)} collective-permute-done((bf16[16,8192]{1,0:T(8,128)(2,1)S(1)}, bf16[16,8192]{1,0:T(8,128)(2,1)S(1)}, u32[]{:S(2)}, u32[]{:S(2)}) %collective-permute-start.1) | collective-permute-done | bytes 262176 | tf_op jit(solution)/shard_map/while/body/eval_jaxpr/ppermute | solution.py:26
  729.7 28.8 %conditional.6 = (bf16[16,8192]{1,0:T(8,128)(2,1)S(1)}, f32[1,131072]{1,0:T(1,128)S(1)}, f32[1,16384]{1,0:T(1,128)S(1)}) conditional(s32[]{:T(128)} %convert_element_type.135, () %tuple.120, (pred[]{:T(512)}, bf16[8,16,8192]{2,1,0:T(8,128)(2,1)}, s32[]{:T(128)}, bf16[16,8192]{1,0:T(8,128)(2,1)S(1)}, f32[8,16,1]{1,2,0:T(1,128)S(1)}, ...), branch_computations={%region_7.7_spmd, %region_8.9_spmd} | conditional | flops 548307520 | bytes 39984272 | solution.py:273
  766.9 28.8 %conditional.6 = (bf16[16,8192]{1,0:T(8,128)(2,1)S(1)}, f32[1,131072]{1,0:T(1,128)S(1)}, f32[1,16384]{1,0:T(1,128)S(1)}) conditional(s32[]{:T(128)} %convert_element_type.135, () %tuple.120, (pred[]{:T(512)}, bf16[8,16,8192]{2,1,0:T(8,128)(2,1)}, s32[]{:T(128)}, bf16[16,8192]{1,0:T(8,128)(2,1)S(1)}, f32[8,16,1]{1,2,0:T(1,128)S(1)}, ...), branch_computations={%region_7.7_spmd, %region_8.9_spmd} | conditional | flops 548307520 | bytes 39984272 | solution.py:273
  804.0 28.8 %conditional.6 = (bf16[16,8192]{1,0:T(8,128)(2,1)S(1)}, f32[1,131072]{1,0:T(1,128)S(1)}, f32[1,16384]{1,0:T(1,128)S(1)}) conditional(s32[]{:T(128)} %convert_element_type.135, () %tuple.120, (pred[]{:T(512)}, bf16[8,16,8192]{2,1,0:T(8,128)(2,1)}, s32[]{:T(128)}, bf16[16,8192]{1,0:T(8,128)(2,1)S(1)}, f32[8,16,1]{1,2,0:T(1,128)S(1)}, ...), branch_computations={%region_7.7_spmd, %region_8.9_spmd} | conditional | flops 548307520 | bytes 39984272 | solution.py:273
  841.1 28.8 %conditional.6 = (bf16[16,8192]{1,0:T(8,128)(2,1)S(1)}, f32[1,131072]{1,0:T(1,128)S(1)}, f32[1,16384]{1,0:T(1,128)S(1)}) conditional(s32[]{:T(128)} %convert_element_type.135, () %tuple.120, (pred[]{:T(512)}, bf16[8,16,8192]{2,1,0:T(8,128)(2,1)}, s32[]{:T(128)}, bf16[16,8192]{1,0:T(8,128)(2,1)S(1)}, f32[8,16,1]{1,2,0:T(1,128)S(1)}, ...), branch_computations={%region_7.7_spmd, %region_8.9_spmd} | conditional | flops 548307520 | bytes 39984272 | solution.py:273
  878.3 28.8 %conditional.6 = (bf16[16,8192]{1,0:T(8,128)(2,1)S(1)}, f32[1,131072]{1,0:T(1,128)S(1)}, f32[1,16384]{1,0:T(1,128)S(1)}) conditional(s32[]{:T(128)} %convert_element_type.135, () %tuple.120, (pred[]{:T(512)}, bf16[8,16,8192]{2,1,0:T(8,128)(2,1)}, s32[]{:T(128)}, bf16[16,8192]{1,0:T(8,128)(2,1)S(1)}, f32[8,16,1]{1,2,0:T(1,128)S(1)}, ...), branch_computations={%region_7.7_spmd, %region_8.9_spmd} | conditional | flops 548307520 | bytes 39984272 | solution.py:273
  915.4 28.8 %conditional.6 = (bf16[16,8192]{1,0:T(8,128)(2,1)S(1)}, f32[1,131072]{1,0:T(1,128)S(1)}, f32[1,16384]{1,0:T(1,128)S(1)}) conditional(s32[]{:T(128)} %convert_element_type.135, () %tuple.120, (pred[]{:T(512)}, bf16[8,16,8192]{2,1,0:T(8,128)(2,1)}, s32[]{:T(128)}, bf16[16,8192]{1,0:T(8,128)(2,1)S(1)}, f32[8,16,1]{1,2,0:T(1,128)S(1)}, ...), branch_computations={%region_7.7_spmd, %region_8.9_spmd} | conditional | flops 548307520 | bytes 39984272 | solution.py:273
  952.6 28.8 %conditional.6 = (bf16[16,8192]{1,0:T(8,128)(2,1)S(1)}, f32[1,131072]{1,0:T(1,128)S(1)}, f32[1,16384]{1,0:T(1,128)S(1)}) conditional(s32[]{:T(128)} %convert_element_type.135, () %tuple.120, (pred[]{:T(512)}, bf16[8,16,8192]{2,1,0:T(8,128)(2,1)}, s32[]{:T(128)}, bf16[16,8192]{1,0:T(8,128)(2,1)S(1)}, f32[8,16,1]{1,2,0:T(1,128)S(1)}, ...), branch_computations={%region_7.7_spmd, %region_8.9_spmd} | conditional | flops 548307520 | bytes 39984272 | solution.py:273
  989.7 28.8 %conditional.6 = (bf16[16,8192]{1,0:T(8,128)(2,1)S(1)}, f32[1,131072]{1,0:T(1,128)S(1)}, f32[1,16384]{1,0:T(1,128)S(1)}) conditional(s32[]{:T(128)} %convert_element_type.135, () %tuple.120, (pred[]{:T(512)}, bf16[8,16,8192]{2,1,0:T(8,128)(2,1)}, s32[]{:T(128)}, bf16[16,8192]{1,0:T(8,128)(2,1)S(1)}, f32[8,16,1]{1,2,0:T(1,128)S(1)}, ...), branch_computations={%region_7.7_spmd, %region_8.9_spmd} | conditional | flops 548307520 | bytes 39984272 | solution.py:273
  1035.7 81.4 %all-to-all-start.2 = ((bf16[32,2,4608]{2,1,0:T(2,128)(2,1)}), bf16[32,2,4608]{2,1,0:T(2,128)(2,1)S(1)}, u32[]{:S(2)}, u32[]{:S(2)}) async-start(bf16[32,2,4608]{2,1,0:T(2,128)(2,1)} %reshape.281), calls=%async_computation.2 | async-start | bytes 1179648 | tf_op jit(solution)/shard_map/all_to_all | solution.py:294
  1117.2 12.0 %all-to-all-done.2 = bf16[32,2,4608]{2,1,0:T(2,128)(2,1)S(1)} async-done(((bf16[32,2,4608]{2,1,0:T(2,128)(2,1)}), bf16[32,2,4608]{2,1,0:T(2,128)(2,1)S(1)}, u32[]{:S(2)}, u32[]{:S(2)}) %all-to-all-start.2) | async-done | bytes 589856 | tf_op jit(solution)/shard_map/all_to_all | solution.py:294
  (441 shorter events, 585.5 us)
Async XLA Ops:
  7.2 274.7 %all-gather.2.cloned.1.call-start = ((), (), s32[]{:S(2)}) async-start(), calls=%async_computation.4 | async-start | bytes 17301504 | tf_op jit(solution)/shard_map/all_gather | solution.py:151
  46.0 235.9 %all-to-all-start.1 = ((bf16[32,1,256,1024]{3,2,1,0:T(8,128)(2,1)}), bf16[32,1,256,1024]{3,2,1,0:T(8,128)(2,1)}, u32[]{:S(2)}, u32[]{:S(2)}) async-start(bf16[32,1,256,1024]{3,2,1,0:T(8,128)(2,1)} %stack.2), calls=%async_computation.1 | async-start | bytes 33554432 | tf_op jit(solution)/shard_map/all_to_all | solution.py:20
  59.9 225.0 %copy-start.2 = (f32[1,8192]{1,0:T(1,128)S(1)}, f32[1,8192]{1,0:T(1,128)}, u32[]{:S(2)}) copy-start(f32[1,8192]{1,0:T(1,128)} %param.24) | copy-start | bytes 98308
  308.5 4.6 collective-permute-start
  336.7 7.1 collective-permute-start
  367.3 7.1 collective-permute-start
  398.0 7.1 collective-permute-start
  428.7 7.1 collective-permute-start
  459.4 7.1 collective-permute-start
  490.0 7.1 collective-permute-start
  520.7 7.1 collective-permute-start
  532.5 26.0 %collective-permute-start = (bf16[16,8192]{1,0:T(8,128)(2,1)S(1)}, bf16[16,8192]{1,0:T(8,128)(2,1)S(1)}, u32[]{:S(2)}, u32[]{:S(2)}) collective-permute-start(bf16[16,8192]{1,0:T(8,128)(2,1)S(1)} %get-tuple-element.992), channel_id=1, source_target_pairs={{0,32},{32,64},{64,96},{1,33},{33,65},{65,97},{2,34},{34,66},{66,9... | collective-permute-start | bytes 786440 | tf_op jit(solution)/shard_map/while/body/eval_jaxpr/ppermute | solution.py:26
  563.1 7.1 collective-permute-start
  574.9 24.1 %collective-permute-start = (bf16[16,8192]{1,0:T(8,128)(2,1)S(1)}, bf16[16,8192]{1,0:T(8,128)(2,1)S(1)}, u32[]{:S(2)}, u32[]{:S(2)}) collective-permute-start(bf16[16,8192]{1,0:T(8,128)(2,1)S(1)} %get-tuple-element.992), channel_id=1, source_target_pairs={{0,32},{32,64},{64,96},{1,33},{33,65},{65,97},{2,34},{34,66},{66,9... | collective-permute-start | bytes 786440 | tf_op jit(solution)/shard_map/while/body/eval_jaxpr/ppermute | solution.py:26
  600.9 7.6 collective-permute-start.1
  610.0 24.8 %collective-permute-start.1 = (bf16[16,8192]{1,0:T(8,128)(2,1)S(1)}, bf16[16,8192]{1,0:T(8,128)(2,1)S(1)}, u32[]{:S(2)}, u32[]{:S(2)}) collective-permute-start(bf16[16,8192]{1,0:T(8,128)(2,1)S(1)} %get-tuple-element.1013), channel_id=1, source_target_pairs={{32,0},{64,32},{96,64},{33,1},{65,33},{97,65},{34,2},{66,34},{98,6... | collective-permute-start | bytes 786440 | tf_op jit(solution)/shard_map/while/body/eval_jaxpr/ppermute | solution.py:26
  636.5 92.0 %collective-permute-start.1 = (bf16[16,8192]{1,0:T(8,128)(2,1)S(1)}, bf16[16,8192]{1,0:T(8,128)(2,1)S(1)}, u32[]{:S(2)}, u32[]{:S(2)}) collective-permute-start(bf16[16,8192]{1,0:T(8,128)(2,1)S(1)} %get-tuple-element.1013), channel_id=1, source_target_pairs={{32,0},{64,32},{96,64},{33,1},{65,33},{97,65},{34,2},{66,34},{98,6... | collective-permute-start | bytes 786440 | tf_op jit(solution)/shard_map/while/body/eval_jaxpr/ppermute | solution.py:26
  758.5 7.1 collective-permute-start.1
  795.6 7.1 collective-permute-start.1
  832.8 7.1 collective-permute-start.1
  869.9 7.1 collective-permute-start.1
  907.1 7.1 collective-permute-start.1
  944.2 7.1 collective-permute-start.1
  981.4 7.1 collective-permute-start.1
  1018.5 7.1 collective-permute-start.1
  1033.3 83.7 %copy-start.11 = (s32[64]{0:T(128)S(1)}, s32[64]{0:T(128)}, u32[]{:S(2)}) copy-start(s32[64]{0:T(128)} %copy-done.10) | copy-start | bytes 772
  1034.4 96.7 %copy-start.13 = (s32[32]{0:T(128)S(1)}, s32[32]{0:T(128)}, u32[]{:S(2)}) copy-start(s32[32]{0:T(128)} %param.27) | copy-start | bytes 388
  1034.4 96.7 %copy-start.15 = (pred[64]{0:T(512)(128)(4,1)S(1)}, pred[64]{0:T(512)(128)(4,1)}, u32[]{:S(2)}) copy-start(pred[64]{0:T(512)(128)(4,1)} %copy-done.14) | copy-start | bytes 196
  1034.4 96.7 %copy-start.16 = (pred[64]{0:T(512)(128)(4,1)S(1)}, pred[64]{0:T(512)(128)(4,1)}, u32[]{:S(2)}) copy-start(pred[64]{0:T(512)(128)(4,1)} %get-tuple-element.797) | copy-start | bytes 196
  1035.7 95.4 %copy-start.3 = (f32[1,64,9216]{2,1,0:T(8,128)S(1)}, f32[1,64,9216]{2,1,0:T(8,128)}, u32[]{:S(2)}) copy-start(f32[1,64,9216]{2,1,0:T(8,128)} %param.33) | copy-start | bytes 7077892
  1035.7 93.6 %all-to-all-start.2 = ((bf16[32,2,4608]{2,1,0:T(2,128)(2,1)}), bf16[32,2,4608]{2,1,0:T(2,128)(2,1)S(1)}, u32[]{:S(2)}, u32[]{:S(2)}) async-start(bf16[32,2,4608]{2,1,0:T(2,128)(2,1)} %reshape.281), calls=%async_computation.2 | async-start | bytes 1179648 | tf_op jit(solution)/shard_map/all_to_all | solution.py:294
  1141.0 15.9 %all-to-all-start.3 = ((bf16[32,2,4608]{2,1,0:T(2,128)(2,1)}), bf16[32,2,4608]{2,1,0:T(2,128)(2,1)S(1)}, u32[]{:S(2)}, u32[]{:S(2)}) async-start(bf16[32,2,4608]{2,1,0:T(2,128)(2,1)} %reshape.283), calls=%async_computation.3 | async-start | bytes 1179648 | tf_op jit(solution)/shard_map/all_to_all | solution.py:314
  (26 other events, 357.7 us)
Sparse Core Ops, SparseCore 0:
  10.2 242.9 all-gather.1
